TPU v7x, 128 devices: a whole 4x4x4 slice. The times are simulated.
128 devices in a mesh: slot: 32 (over y, z, core), hid: 4 (over x).
Axes of the slice: x: 4, y: 4, z: 4, core: 2. Of those that a mesh axis runs over, the one named last changes fastest.
Arguments:
- master: float32 [16, 3, 4, 393216], P(None, None, 'hid', 'slot'), may hold values from -0.125 to 0.125
- first_moment: float32 [16, 3, 4, 393216], P(None, None, 'hid', 'slot'), may hold values from -0.3 to 0.3
- second_moment: float32 [16, 3, 4, 393216], P(None, None, 'hid', 'slot'), may hold values from 0.0001 to 0.01
- slot_weights: bfloat16 [32, 3, 768, 2048], P('slot', None, 'hid'), may hold values from -0.125 to 0.125
- back_rows: bfloat16 [32, 1024, 2048], P('slot'), may hold values from -6 to 6
- readout: bfloat16 [32, 1024, 2048], P('slot'), may hold values from -0.25 to 0.25
- ref_logratio: float32 [32, 1024], P('slot'), may hold values from -9 to 0
- labels: int32 [32, 1024], P('slot'), may hold values 0 or 1
- place_cur: int32 [32], replicated, may hold values from 0 to 15, as said below
- place_next: int32 [32], replicated, may hold values from 0 to 15, as said below
- fwd_rows: bfloat16 [8192, 2048], P('slot', 'hid'), may hold values from -6 to 6
- routes: int32 [8192, 1], P('slot'), may hold values from 0 to 31; in each aligned block of 256 rows (0 to 255, 256 to 511, ...) at most 16 rows name the same one
Outputs:
- out_rows: bfloat16 [8192, 2048], P('slot', 'hid')
- new_master: float32 [16, 3, 4, 393216], P(None, None, 'hid', 'slot')
- new_first: float32 [16, 3, 4, 393216], P(None, None, 'hid', 'slot')
- new_second: float32 [16, 3, 4, 393216], P(None, None, 'hid', 'slot')
Inputs may be any that keep to these rules, and one draw needn't show every extreme that they name: `place_cur`: every expert 0 to 15 is held by at least one slot. `place_next`: every expert 0 to 15 is held by at least one slot. `routes`: the rows of one slot name any one slot at most 16 times, a bound that some block reaches.
All inputs are finite; a program needn't handle non-finite values. No bound on the sum of `labels` on one device may be relied on, other than what follows from the above.
Results may differ from a plain program's by a relative error of at most 0.008.
Values may be sent and summed in bfloat16 or wider, within the bound.
No kernel may reach another device: no remote copies, remote signals or barrier semaphores. Data moves between devices by JAX's collectives and lax.ppermute only.
A program may use at most 128 MiB of HBM per device.

v0:
```python
import jax
import jax.numpy as jnp
from jax import lax
from jax.sharding import PartitionSpec as P

beta_kto = 1.0
desired_weight = 1.0
undesired_weight = 1.33
learn_rate = 0.004
decay_first = 0.9
decay_second = 0.999
correct_first = 0.9999734386011124
correct_second = 0.09520785288629043
adam_eps = 1e-08
weight_decay = 0.1


def expert_pass(inputs, weights):
    across = (((1,), (1,)), ((), ()))
    gate_vals = lax.dot_general(inputs, weights[0], across, preferred_element_type=jnp.float32)
    up_vals = lax.dot_general(inputs, weights[1], across, preferred_element_type=jnp.float32)
    hidden = (gate_vals * jax.nn.sigmoid(gate_vals) * up_vals).astype(jnp.bfloat16)
    produced = jnp.dot(hidden, weights[2], preferred_element_type=jnp.float32)
    return (gate_vals, up_vals, hidden, produced)


def kto_slope(scores, labels, center):
    sigma_v = jax.nn.sigmoid(beta_kto * (scores - center))
    signed = jnp.where(labels == 1, -desired_weight, undesired_weight)
    return beta_kto * sigma_v * (1.0 - sigma_v) * signed


def expert_backward(inputs, direction, weights, slope, gate_vals, up_vals, hidden):
    d_expert = (slope[:, None] * direction.astype(jnp.float32)).astype(jnp.bfloat16)
    d_hidden = lax.dot_general(
        d_expert, weights[2], (((1,), (1,)), ((), ())), preferred_element_type=jnp.float32
    )
    sigma_g = jax.nn.sigmoid(gate_vals)
    d_gate = (d_hidden * up_vals * sigma_g * (1.0 + gate_vals * (1.0 - sigma_g))).astype(
        jnp.bfloat16
    )
    d_up = (d_hidden * gate_vals * sigma_g).astype(jnp.bfloat16)
    contract = (((0,), (0,)), ((), ()))
    grad_gate = lax.dot_general(d_gate, inputs, contract, preferred_element_type=jnp.float32)
    grad_up = lax.dot_general(d_up, inputs, contract, preferred_element_type=jnp.float32)
    grad_down = lax.dot_general(hidden, d_expert, contract, preferred_element_type=jnp.float32)
    return jnp.stack([grad_gate, grad_up, grad_down])


def adamw_update(master, first_moment, second_moment, summed):
    new_first = decay_first * first_moment + (1.0 - decay_first) * summed
    new_second = decay_second * second_moment + (1.0 - decay_second) * summed * summed
    update = new_first / correct_first / (jnp.sqrt(new_second / correct_second) + adam_eps)
    new_master = master - learn_rate * (update + weight_decay * master)
    return (new_master, new_first, new_second)


def shards(
    master,
    first_moment,
    second_moment,
    slot_weights,
    back_rows,
    readout,
    ref_logratio,
    labels,
    place_cur,
    place_next,
    fwd_rows,
    routes,
):
    slot_count = lax.axis_size("slot")
    experts_here = master.shape[0]
    weights = slot_weights[0]
    width = weights.shape[2]
    owned_units = master.shape[3] // width
    inputs = back_rows[0]
    direction = readout[0]
    gate_vals, up_vals, hidden, partial_value = expert_pass(inputs, weights)
    row_part = jnp.sum(partial_value * direction.astype(jnp.float32), axis=1)
    policy = lax.psum(row_part, "hid")
    scores = policy - ref_logratio[0]
    row_total = slot_count * inputs.shape[0]
    center = lax.psum(jnp.sum(scores), "slot") / row_total
    slope = kto_slope(scores, labels[0], center)
    grads = expert_backward(inputs, direction, weights, slope, gate_vals, up_vals, hidden)
    arrived = lax.all_to_all(
        grads[None].astype(jnp.bfloat16), "slot", split_axis=2, concat_axis=0, tiled=True
    ).astype(jnp.float32)
    arrived = arrived.reshape(slot_count, 3, 1, owned_units * width)
    owner_map = (place_cur[None, :] == jnp.arange(experts_here, dtype=jnp.int32)[:, None]).astype(
        jnp.float32
    )
    summed = jnp.einsum("es,sabc->eabc", owner_map, arrived, precision=lax.Precision.HIGHEST)
    new_master, new_first, new_second = adamw_update(master, first_moment, second_moment, summed)
    refreshed = new_master.astype(jnp.bfloat16)
    pick_map = (place_next[:, None] == jnp.arange(experts_here, dtype=jnp.int32)[None, :]).astype(
        jnp.bfloat16
    )
    picked = jnp.einsum(
        "se,eabc->sabc", pick_map, refreshed, preferred_element_type=jnp.float32
    ).astype(jnp.bfloat16)
    picked = picked.reshape(slot_count, 3, owned_units, width)
    resident = lax.all_to_all(picked, "slot", split_axis=0, concat_axis=2, tiled=True)[0]
    capacity = 2 * fwd_rows.shape[0] // slot_count
    quarter = fwd_rows.shape[1]
    target = routes[:, 0]
    target_map = (target[:, None] == jnp.arange(slot_count, dtype=jnp.int32)[None, :]).astype(
        jnp.int32
    )
    earlier = jnp.cumsum(target_map, axis=0) - target_map
    position = jnp.sum(earlier * target_map, axis=1)
    slot_place = target * capacity + position
    place_map = (
        slot_place[None, :] == jnp.arange(slot_count * capacity, dtype=jnp.int32)[:, None]
    ).astype(jnp.bfloat16)
    widened = lax.all_gather(fwd_rows, "hid", axis=1, tiled=True)
    buffer_rows = jnp.dot(place_map, widened, preferred_element_type=jnp.float32).astype(
        jnp.bfloat16
    )
    buffer_rows = buffer_rows.reshape(slot_count, capacity, widened.shape[1])
    arrived_rows = lax.all_to_all(
        buffer_rows, "slot", split_axis=0, concat_axis=0, tiled=True
    ).reshape(slot_count * capacity, widened.shape[1])
    fwd_partial = expert_pass(arrived_rows, resident)[3]
    totals = lax.psum(fwd_partial, "hid")
    shares = lax.dynamic_slice_in_dim(totals, lax.axis_index("hid") * quarter, quarter, 1)
    outgoing = shares.astype(jnp.bfloat16).reshape(slot_count, capacity, quarter)
    returned = lax.all_to_all(outgoing, "slot", split_axis=0, concat_axis=0, tiled=True).reshape(
        slot_count * capacity, quarter
    )
    out_rows = lax.dot_general(
        place_map, returned, (((0,), (0,)), ((), ())), preferred_element_type=jnp.float32
    ).astype(jnp.bfloat16)
    return (out_rows, new_master, new_first, new_second)


def solution(mesh):
    return jax.shard_map(
        shards,
        mesh=mesh,
        in_specs=(
            P(None, None, "hid", "slot"),
            P(None, None, "hid", "slot"),
            P(None, None, "hid", "slot"),
            P("slot", None, "hid", None),
            P("slot", None, None),
            P("slot", None, None),
            P("slot", None),
            P("slot", None),
            P(),
            P(),
            P("slot", "hid"),
            P("slot", None),
        ),
        out_specs=(
            P("slot", "hid"),
            P(None, None, "hid", "slot"),
            P(None, None, "hid", "slot"),
            P(None, None, "hid", "slot"),
        ),
        check_vma=False,
    )
```

profile of v0, /device:TPU:1, one launch (start us, length us, event | category | flops | bytes accessed | tf_op | source)
XLA Modules:
  0.0 364.6 jit_solution(15891182138285590733)
XLA Ops:
  7.2 0.0 copy-start.11
  7.2 0.0 copy-start.13
  7.2 4.1 %fusion.16 = f32[1024,192]{0,1:T(8,128)S(1)} fusion(bf16[1,1024,2048]{2,1,0:T(8,128)(2,1)} %param.16, bf16[1,3,192,2048]{3,2,1,0:T(8,128)(2,1)} %param.15), kind=kOutput, calls=%fused_computation.17 | convolution fusion | flops 805306368 | bytes 5767168 | tf_op jit(solution)/shard_map/dot_general | solution.py:20
  11.3 0.0 copy-done.11
  11.3 0.3 copy-done.13
  11.6 2.5 multiply_convert_fusion.2
  14.1 0.0 copy-done.9
  14.1 1.4 fusion.2
  15.5 9.3 %psum.21 = f32[1024]{0:T(1024)S(1)} all-reduce(f32[1024]{0:T(1024)S(1)} %fusion.2), channel_id=1, replica_groups=mesh['slot'=32,'hid'=4] {'hid'}, use_global_device_ids=true, to_apply=%region_4.5 | all-reduce | flops 1024 | bytes 8192 | tf_op jit(solution)/shard_map/psum | solution.py:81
  24.8 0.0 copy-done.6
  24.8 0.6 fusion.78
  25.4 66.9 %psum.22 = f32[]{:T(128)} all-reduce(f32[]{:T(128)} %get-tuple-element.19), channel_id=1, replica_groups=mesh['slot'=32,'hid'=4] {'slot'}, use_global_device_ids=true, to_apply=%region_6.7 | all-reduce | flops 1 | bytes 8 | tf_op jit(solution)/shard_map/psum | solution.py:84
  92.3 0.0 copy-done.7
  93.0 0.0 copy-start.10
  93.0 4.0 %fusion.6 = f32[1024,192]{0,1:T(8,128)S(1)} fusion(bf16[1,1024,2048]{2,1,0:T(8,128)(2,1)} %param.17, f32[1024]{0:T(1024)S(1)} %fusion.71, bf16[1,3,192,2048]{3,2,1,0:T(8,128)(2,1)S(1)} %copy-done.13), kind=kOutput, calls=%fused_computation.9 | convolution fusion | flops 811597824 | bytes 5771264 | tf_op jit(solution)/shard_map/dot_general | solution.py:35
  96.9 0.0 copy-done.10
  96.9 0.0 copy-start.12
  96.9 1.2 fusion.35
  98.1 1.0 copy-done.12
  99.1 1.1 fusion.29
  100.2 0.1 copy-done.15
  100.3 1.2 fusion.32
  101.5 0.3 pad_maximum_fusion
  101.7 2.0 copy.33
  103.8 45.2 %all_to_all.40 = bf16[1,3,192,2048]{3,1,0,2:T(4,128)(2,1)S(1)} all-to-all(bf16[1,3,192,2048]{3,1,0,2:T(4,128)(2,1)S(1)} %copy.33), channel_id=1, replica_groups=mesh['slot'=32,'hid'=4] {'slot'}, dimensions={2} | all-to-all | bytes 4718592 | tf_op jit(solution)/shard_map/all_to_all | solution.py:87
  148.9 1.7 copy.55
  150.6 0.0 copy-start.14
  150.7 4.5 %reshape.144 = bf16[32,3,12288]{2,0,1:T(8,128)(2,1)} reshape(bf16[32,1,3,6,2048]{4,3,0,2,1:T(8,128)(2,1)S(1)} %bitcast.131) | data formatting | bytes 4718592 | tf_op jit(solution)/shard_map/reshape.20
  155.2 0.0 copy-done.14
  155.2 11.4 %multiply_subtract_fusion = (f32[16,3,1,12288]{3,0,1,2:T(8,128)S(1)}, f32[16,3,1,12288]{3,0,1,2:T(8,128)}, f32[16,3,1,12288]{3,0,1,2:T(8,128)}) fusion(f32[16,3,1,12288]{3,2,1,0:T(1,128)} %param.12, f32[16,3,1,12288]{3,2,1,0:T(1,128)} %param.13, f32[16,3,1,12288]{3,2,1,0:T(1,128)} %param.14, bf16[32,3,12288]{2,0,1:T(8,128)(2,1)} %reshape.144, ...), kind=kOutput, calls=%fused_computation.36 | convolution fusion | flops 46596608 | bytes 16515200 | tf_op jit(solution)/shard_map/es,sabc->eabc/dot_general | solution.py:94
  166.5 1.4 copy-done
  167.9 0.0 copy-done.8
  167.9 2.2 convolution_convert_fusion
  170.2 5.0 %reshape.146 = bf16[32,3,6,2048]{3,2,0,1:T(8,128)(2,1)S(1)} reshape(bf16[32,3,12288]{2,0,1:T(8,128)(2,1)} %convolution_convert_fusion) | data formatting | bytes 4718592 | tf_op jit(solution)/shard_map/reshape | solution.py:103
  175.1 1.9 copy.38
  177.0 4.0 %all-to-all-start.2 = ((bf16[32,3,6,2048]{3,2,1,0:T(8,128)(2,1)}), bf16[32,3,6,2048]{3,2,1,0:T(8,128)(2,1)S(1)}, u32[]{:S(2)}, u32[]{:S(2)}) async-start(bf16[32,3,6,2048]{3,2,1,0:T(8,128)(2,1)} %copy.38), calls=%async_computation.2 | async-start | bytes 6291456 | tf_op jit(solution)/shard_map/all_to_all | solution.py:104
  181.1 0.0 all-gather.2.cloned.1.call-start
  181.1 0.7 all-gather.2.cloned.1.call-update
  181.8 0.0 copy-done.5
  181.8 0.6 reduce-window.6
  182.4 0.2 slice_reduce_fusion
  182.6 0.1 fusion.64
  182.8 21.8 %all-gather.2.cloned.1.call-done = bf16[256,2048]{1,0:T(8,128)(2,1)} async-done(((bf16[256,512]{1,0:T(8,128)(2,1)}), bf16[256,2048]{1,0:T(8,128)(2,1)}) %all-gather.2.cloned.1.call-update) | async-done | bytes 1048592 | tf_op jit(solution)/shard_map/all_gather | solution.py:117
  204.6 3.3 convolution_convert_fusion.1
  207.9 13.0 %all-to-all-done.2 = bf16[32,3,6,2048]{3,2,1,0:T(8,128)(2,1)S(1)} async-done(((bf16[32,3,6,2048]{3,2,1,0:T(8,128)(2,1)}), bf16[32,3,6,2048]{3,2,1,0:T(8,128)(2,1)S(1)}, u32[]{:S(2)}, u32[]{:S(2)}) %all-to-all-start.2) | async-done | bytes 2359328 | tf_op jit(solution)/shard_map/all_to_all | solution.py:104
  220.8 5.3 %all-to-all-start = ((bf16[32,16,2048]{2,1,0:T(8,128)(2,1)}), bf16[32,16,2048]{2,1,0:T(8,128)(2,1)}, u32[]{:S(2)}, u32[]{:S(2)}) async-start(bf16[32,16,2048]{2,1,0:T(8,128)(2,1)} %bitcast.132), calls=%async_computation | async-start | bytes 4194304 | tf_op jit(solution)/shard_map/all_to_all | solution.py:122
  226.1 1.8 fusion.79
  227.9 1.5 squeeze.38
  229.4 1.4 squeeze.39
  230.8 0.3 squeeze.40
  231.0 23.5 %all-to-all-done = bf16[32,16,2048]{2,1,0:T(8,128)(2,1)} async-done(((bf16[32,16,2048]{2,1,0:T(8,128)(2,1)}), bf16[32,16,2048]{2,1,0:T(8,128)(2,1)}, u32[]{:S(2)}, u32[]{:S(2)}) %all-to-all-start) | async-done | bytes 2097184 | tf_op jit(solution)/shard_map/all_to_all | solution.py:122
  254.6 2.4 fusion.80
  257.0 5.1 %fusion.43 = f32[512,2048]{1,0:T(8,128)} fusion(bf16[192,2048]{1,0:T(8,128)(2,1)S(1)} %squeeze.40, bf16[512,2048]{1,0:T(8,128)(2,1)} %bitcast.4, bf16[192,2048]{1,0:T(8,128)(2,1)S(1)} %squeeze.39, f32[512,192]{0,1:T(8,128)S(1)} %fusion.80), kind=kOutput, calls=%fused_computation.42 | convolution fusion | flops 805896192 | bytes 8257536 | tf_op jit(solution)/shard_map/dot_general | solution.py:23
  262.1 75.4 %all-reduce.1 = bf16[512,2048]{1,0:T(8,128)(2,1)} all-reduce(f32[512,2048]{1,0:T(8,128)} %fusion.43), channel_id=1, replica_groups=mesh['slot'=32,'hid'=4] {'hid'}, use_global_device_ids=true, to_apply=%region_7.8 | all-reduce | flops 1048576 | bytes 6291456 | tf_op jit(solution)/shard_map/psum | solution.py:126
  337.6 1.9 dynamic-slice_convert_fusion
  339.4 5.5 %all-to-all-start.3 = ((bf16[32,16,512]{2,1,0:T(8,128)(2,1)}), bf16[32,16,512]{2,1,0:T(8,128)(2,1)S(1)}, u32[]{:S(2)}, u32[]{:S(2)}) async-start(bf16[32,16,512]{2,1,0:T(8,128)(2,1)} %bitcast.26), calls=%async_computation.3 | async-start | bytes 1048576 | tf_op jit(solution)/shard_map/all_to_all | solution.py:129
  345.0 0.0 copy-start.4
  345.0 3.8 %copy.39 = f32[16,3,1,12288]{3,2,1,0:T(1,128)} copy(f32[16,3,1,12288]{3,0,1,2:T(8,128)S(1)} %copy-done.1) | data formatting | bytes 4718592
  348.8 0.0 copy-done.4
  348.8 3.8 %copy.40 = f32[16,3,1,12288]{3,2,1,0:T(1,128)} copy(f32[16,3,1,12288]{3,0,1,2:T(8,128)S(1)} %copy-done.4) | data formatting | bytes 4718592
  352.7 0.0 copy-done.3
  352.7 3.8 %copy.41 = f32[16,3,1,12288]{3,2,1,0:T(1,128)} copy(f32[16,3,1,12288]{3,0,1,2:T(8,128)S(1)} %copy-done.3) | data formatting | bytes 4718592
  356.5 0.2 all-to-all-done.3
  356.7 1.1 convolution_convert_fusion.2
  (18 shorter events, 0.1 us)
Async XLA Ops:
  7.2 4.1 %copy-start.11 = (bf16[1,1024,2048]{2,1,0:T(8,128)(2,1)S(1)}, bf16[1,1024,2048]{2,1,0:T(8,128)(2,1)}, u32[]{:S(2)}) copy-start(bf16[1,1024,2048]{2,1,0:T(8,128)(2,1)} %param.16) | copy-start | bytes 12582916
  7.2 4.4 %copy-start.13 = (bf16[1,3,192,2048]{3,2,1,0:T(8,128)(2,1)S(1)}, bf16[1,3,192,2048]{3,2,1,0:T(8,128)(2,1)}, u32[]{:S(2)}) copy-start(bf16[1,3,192,2048]{3,2,1,0:T(8,128)(2,1)} %param.15) | copy-start | bytes 7077892
  11.6 2.5 copy-start.9
  14.1 10.7 %copy-start.6 = (f32[1,1024]{1,0:T(1,128)S(1)}, f32[1,1024]{1,0:T(1,128)}, u32[]{:S(2)}) copy-start(f32[1,1024]{1,0:T(1,128)} %param.18) | copy-start | bytes 12292
  14.1 78.2 %copy-start.7 = (s32[1,1024]{1,0:T(1,128)S(1)}, s32[1,1024]{1,0:T(1,128)}, u32[]{:S(2)}) copy-start(s32[1,1024]{1,0:T(1,128)} %param.19) | copy-start | bytes 12292
  93.0 4.0 %copy-start.10 = (bf16[1,1024,2048]{2,1,0:T(8,128)(2,1)S(1)}, bf16[1,1024,2048]{2,1,0:T(8,128)(2,1)}, u32[]{:S(2)}) copy-start(bf16[1,1024,2048]{2,1,0:T(8,128)(2,1)} %param.17) | copy-start | bytes 12582916
  96.9 2.2 copy-start.12
  99.1 1.1 copy-start.15
  150.6 4.5 %copy-start.14 = (s32[32]{0:T(128)S(1)}, s32[32]{0:T(128)}, u32[]{:S(2)}) copy-start(s32[32]{0:T(128)} %param.20) | copy-start | bytes 388
  155.2 12.8 %copy-start.8 = (s32[32]{0:T(128)S(1)}, s32[32]{0:T(128)}, u32[]{:S(2)}) copy-start(s32[32]{0:T(128)} %param.21) | copy-start | bytes 388
  166.5 1.4 copy-start
  177.0 4.8 %copy-start.5 = (s32[256,1]{0,1:T(1,128)S(1)}, s32[256,1]{0,1:T(1,128)}, u32[]{:S(2)}) copy-start(s32[256,1]{0,1:T(1,128)} %param.23) | copy-start | bytes 3076
  177.0 43.8 %all-to-all-start.2 = ((bf16[32,3,6,2048]{3,2,1,0:T(8,128)(2,1)}), bf16[32,3,6,2048]{3,2,1,0:T(8,128)(2,1)S(1)}, u32[]{:S(2)}, u32[]{:S(2)}) async-start(bf16[32,3,6,2048]{3,2,1,0:T(8,128)(2,1)} %copy.38), calls=%async_computation.2 | async-start | bytes 6291456 | tf_op jit(solution)/shard_map/all_to_all | solution.py:104
  181.1 23.5 %all-gather.2.cloned.1.call-start = ((), (), s32[]{:S(2)}) async-start(), calls=%async_computation.4 | async-start | bytes 1310720 | tf_op jit(solution)/shard_map/all_gather | solution.py:117
  220.8 33.7 %all-to-all-start = ((bf16[32,16,2048]{2,1,0:T(8,128)(2,1)}), bf16[32,16,2048]{2,1,0:T(8,128)(2,1)}, u32[]{:S(2)}, u32[]{:S(2)}) async-start(bf16[32,16,2048]{2,1,0:T(8,128)(2,1)} %bitcast.132), calls=%async_computation | async-start | bytes 4194304 | tf_op jit(solution)/shard_map/all_to_all | solution.py:122
  227.9 2.9 copy-start.2
  262.1 82.8 %copy-start.1 = (f32[16,3,1,12288]{3,0,1,2:T(8,128)S(1)}, f32[16,3,1,12288]{3,0,1,2:T(8,128)}, u32[]{:S(2)}) copy-start(f32[16,3,1,12288]{3,0,1,2:T(8,128)} %copy-done) | copy-start | bytes 7077892
  339.4 17.2 %all-to-all-start.3 = ((bf16[32,16,512]{2,1,0:T(8,128)(2,1)}), bf16[32,16,512]{2,1,0:T(8,128)(2,1)S(1)}, u32[]{:S(2)}, u32[]{:S(2)}) async-start(bf16[32,16,512]{2,1,0:T(8,128)(2,1)} %bitcast.26), calls=%async_computation.3 | async-start | bytes 1048576 | tf_op jit(solution)/shard_map/all_to_all | solution.py:129
  345.0 3.8 %copy-start.4 = (f32[16,3,1,12288]{3,0,1,2:T(8,128)S(1)}, f32[16,3,1,12288]{3,0,1,2:T(8,128)}, u32[]{:S(2)}) copy-start(f32[16,3,1,12288]{3,0,1,2:T(8,128)} %get-tuple-element.17) | copy-start | bytes 7077892
  348.8 3.8 %copy-start.3 = (f32[16,3,1,12288]{3,0,1,2:T(8,128)S(1)}, f32[16,3,1,12288]{3,0,1,2:T(8,128)}, u32[]{:S(2)}) copy-start(f32[16,3,1,12288]{3,0,1,2:T(8,128)} %get-tuple-element.18) | copy-start | bytes 7077892
Sparse Core Ops, SparseCore 0:
  183.5 21.0 all-gather.1
where the time goes:
time: 365 us
  blocking collectives  197 us (54%)
  waiting for transfers between devices  59.2 us (16%)
  matrix products  40.8 us (11%)
  local copies, waits for them, and re-layouts  36.4 us (10%)
  starting transfers between devices  14.9 us (4%)
  between operations  14.9 us (4%)
    psum x1, blocking collectives, shards(): totals = lax.psum(fwd_partial, 'hid')  75.4 us
    psum x1, blocking collectives, shards(): center = lax.psum(jnp.sum(scores), 'slot') / row_total  66.9 us
    all_to_all x1, blocking collectives, shards(): lax.all_to_all(grads[None].astype(jnp.bfloat16), 'slot', split_axis=2, co...  45.2 us
    all_to_all x1, waiting for transfers between devices, shards(): lax.all_to_all(buffer_rows, 'slot', split_axis=0, concat_axis=0, tiled=True)  23.5 us
    all_gather x1, waiting for transfers between devices, shards(): widened = lax.all_gather(fwd_rows, 'hid', axis=1, tiled=True)  21.8 us
    unnamed x35, local copies, waits for them, and re-layouts  14.4 us
    all_to_all x1, waiting for transfers between devices, shards(): lax.all_to_all(picked, 'slot', split_axis=0, concat_axis=2, tiled=True)[0]  13 us
    dot_general x1, matrix products, shards(): jnp.einsum('es,sabc->eabc', owner_map, arrived, precision=lax.Precision.H...  11.4 us
  transfers between devices with their start and end apart: 4, of which 4 were waited for; matrix products, arithmetic and copies ran while one was open for 6% of the time, Pallas kernels for 0%

commit v1 on v0

--- a/solution.py
+++ b/solution.py
@@ -123,7 +123,7 @@
         buffer_rows, "slot", split_axis=0, concat_axis=0, tiled=True
     ).reshape(slot_count * capacity, widened.shape[1])
     fwd_partial = expert_pass(arrived_rows, resident)[3]
-    totals = lax.psum(fwd_partial, "hid")
+    totals = jnp.sum(lax.all_gather(fwd_partial, "hid"), axis=0)
     shares = lax.dynamic_slice_in_dim(totals, lax.axis_index("hid") * quarter, quarter, 1)
     outgoing = shares.astype(jnp.bfloat16).reshape(slot_count, capacity, quarter)
     returned = lax.all_to_all(outgoing, "slot", split_axis=0, concat_axis=0, tiled=True).reshape(

time: 365 us -> 460 us (1.26); the launches traced: 365 us -> 451 us
  waiting for transfers between devices: 59.2 us -> 208 us
  blocking collectives: 197 us -> 122 us
  other arithmetic: 1.62 us -> 11.4 us
    all_gather x0 -> x1, waiting for transfers between devices: none -> 149 us  [shards(): totals = jnp.sum(lax.all_gather(fwd_partial, 'hid'), axis=0)]
    psum x1 -> x0, blocking collectives: 75.4 us -> none  [shards(): totals = lax.psum(fwd_partial, 'hid')]
    reduce_sum x0 -> x1, other arithmetic: none -> 9.83 us  [shards(): totals = jnp.sum(lax.all_gather(fwd_partial, 'hid'), axis=0)]
  transfers between devices with their start and end apart: 4 -> 5, of which waited for: 4 -> 4; matrix products, arithmetic and copies ran while one was open for 6% -> 5% of each run, Pallas kernels for 0% -> 0%
where the time goes in v1:
time: 460 us; the launch traced here: 451 us
  waiting for transfers between devices  208 us (45%)
  blocking collectives  122 us (27%)
  matrix products  40.8 us (9%)
  local copies, waits for them, and re-layouts  36.4 us (8%)
  starting transfers between devices  17.5 us (4%)
  between operations  15.2 us (3%)
  other arithmetic  11.4 us (2%)
    all_gather x1, waiting for transfers between devices, shards(): totals = jnp.sum(lax.all_gather(fwd_partial, 'hid'), axis=0)  149 us
    psum x1, blocking collectives, shards(): center = lax.psum(jnp.sum(scores), 'slot') / row_total  66.9 us
    all_to_all x1, blocking collectives, shards(): lax.all_to_all(grads[None].astype(jnp.bfloat16), 'slot', split_axis=2, co...  45.6 us
    all_to_all x1, waiting for transfers between devices, shards(): lax.all_to_all(buffer_rows, 'slot', split_axis=0, concat_axis=0, tiled=True)  23.5 us
    all_gather x1, waiting for transfers between devices, shards(): widened = lax.all_gather(fwd_rows, 'hid', axis=1, tiled=True)  21.9 us
    unnamed x35, local copies, waits for them, and re-layouts  14.4 us
    all_to_all x1, waiting for transfers between devices, shards(): lax.all_to_all(picked, 'slot', split_axis=0, concat_axis=2, tiled=True)[0]  13 us
    dot_general x1, matrix products, shards(): jnp.einsum('es,sabc->eabc', owner_map, arrived, precision=lax.Precision.H...  11.3 us
  transfers between devices with their start and end apart: 5, of which 4 were waited for; matrix products, arithmetic and copies ran while one was open for 5% of the time, Pallas kernels for 0%

profile of v1, /device:TPU:1, one launch (start us, length us, event | category | flops | bytes accessed | tf_op | source)
XLA Modules:
  0.0 451.4 jit_solution(15257622905434706416)
XLA Ops:
  7.2 0.0 copy-start.11
  7.2 0.0 copy-start.13
  7.2 4.1 fusion.16
  11.3 0.0 copy-done.11
  11.3 0.3 copy-done.13
  11.6 2.5 multiply_convert_fusion.2
  14.1 1.4 fusion.2
  15.5 9.3 %psum.14 = f32[1024]{0:T(1024)S(1)} all-reduce(f32[1024]{0:T(1024)S(1)} %fusion.2), channel_id=1, replica_groups=mesh['slot'=32,'hid'=4] {'hid'}, use_global_device_ids=true, to_apply=%region_4.5 | all-reduce | flops 1024 | bytes 8192 | tf_op jit(solution)/shard_map/psum | solution.py:81
  24.8 0.0 copy-done.6
  24.8 0.6 fusion.78
  25.4 66.9 %psum.15 = f32[]{:T(128)} all-reduce(f32[]{:T(128)} %get-tuple-element.19), channel_id=1, replica_groups=mesh['slot'=32,'hid'=4] {'slot'}, use_global_device_ids=true, to_apply=%region_6.7 | all-reduce | flops 1 | bytes 8 | tf_op jit(solution)/shard_map/psum | solution.py:84
  92.3 0.0 copy-done.7
  93.0 0.0 copy-start.10
  93.0 4.0 fusion.6
  96.9 0.0 copy-start.12
  96.9 1.2 fusion.35
  98.1 1.0 copy-done.12
  99.1 1.1 fusion.29
  100.2 0.1 copy-done.15
  100.3 1.2 fusion.32
  101.5 0.3 pad_maximum_fusion
  101.7 2.0 copy.33
  103.8 45.6 %all_to_all.40 = bf16[1,3,192,2048]{3,1,0,2:T(4,128)(2,1)S(1)} all-to-all(bf16[1,3,192,2048]{3,1,0,2:T(4,128)(2,1)S(1)} %copy.33), channel_id=1, replica_groups=mesh['slot'=32,'hid'=4] {'slot'}, dimensions={2} | all-to-all | bytes 4718592 | tf_op jit(solution)/shard_map/all_to_all | solution.py:87
  149.4 1.7 copy.55
  151.1 0.0 copy-start.14
  151.1 4.5 %reshape.144 = bf16[32,3,12288]{2,0,1:T(8,128)(2,1)} reshape(bf16[32,1,3,6,2048]{4,3,0,2,1:T(8,128)(2,1)S(1)} %bitcast.133) | data formatting | bytes 4718592 | tf_op jit(solution)/shard_map/reshape.20
  155.7 0.0 copy-done.14
  155.7 11.3 %multiply_subtract_fusion = (f32[16,3,1,12288]{3,0,1,2:T(8,128)S(1)}, f32[16,3,1,12288]{3,0,1,2:T(8,128)}, f32[16,3,1,12288]{3,0,1,2:T(8,128)}) fusion(f32[16,3,1,12288]{3,2,1,0:T(1,128)} %param.12, f32[16,3,1,12288]{3,2,1,0:T(1,128)} %param.13, f32[16,3,1,12288]{3,2,1,0:T(1,128)} %param.14, bf16[32,3,12288]{2,0,1:T(8,128)(2,1)} %reshape.144, ...), kind=kOutput, calls=%fused_computation.36 | convolution fusion | flops 46596608 | bytes 16515200 | tf_op jit(solution)/shard_map/es,sabc->eabc/dot_general | solution.py:94
  167.0 1.4 copy-done
  168.4 0.0 copy-done.8
  168.4 2.2 convolution_convert_fusion
  170.6 5.0 %reshape.146 = bf16[32,3,6,2048]{3,2,0,1:T(8,128)(2,1)S(1)} reshape(bf16[32,3,12288]{2,0,1:T(8,128)(2,1)} %convolution_convert_fusion) | data formatting | bytes 4718592 | tf_op jit(solution)/shard_map/reshape | solution.py:103
  175.6 1.9 copy.38
  177.5 4.0 all-to-all-start.2
  181.5 0.0 all-gather.4.cloned.1.call-start
  181.6 0.7 all-gather.4.cloned.1.call-update
  182.3 0.0 copy-done.5
  182.3 0.6 reduce-window.6
  182.9 0.2 slice_reduce_fusion
  183.1 0.1 fusion.64
  183.2 21.9 %all-gather.4.cloned.1.call-done = bf16[256,2048]{1,0:T(8,128)(2,1)} async-done(((bf16[256,512]{1,0:T(8,128)(2,1)}), bf16[256,2048]{1,0:T(8,128)(2,1)}) %all-gather.4.cloned.1.call-update) | async-done | bytes 1048592 | tf_op jit(solution)/shard_map/all_gather | solution.py:117
  205.1 3.3 convolution_convert_fusion.1
  208.4 13.0 %all-to-all-done.2 = bf16[32,3,6,2048]{3,2,1,0:T(8,128)(2,1)S(1)} async-done(((bf16[32,3,6,2048]{3,2,1,0:T(8,128)(2,1)}), bf16[32,3,6,2048]{3,2,1,0:T(8,128)(2,1)S(1)}, u32[]{:S(2)}, u32[]{:S(2)}) %all-to-all-start.2) | async-done | bytes 2359328 | tf_op jit(solution)/shard_map/all_to_all | solution.py:104
  221.3 5.2 %all-to-all-start = ((bf16[32,16,2048]{2,1,0:T(8,128)(2,1)}), bf16[32,16,2048]{2,1,0:T(8,128)(2,1)}, u32[]{:S(2)}, u32[]{:S(2)}) async-start(bf16[32,16,2048]{2,1,0:T(8,128)(2,1)} %bitcast.134), calls=%async_computation | async-start | bytes 4194304 | tf_op jit(solution)/shard_map/all_to_all | solution.py:122
  226.6 0.0 all-gather.6.cloned.1.call-start
  226.6 1.7 fusion.79
  228.3 1.5 squeeze.38
  229.8 1.4 squeeze.39
  231.3 0.3 squeeze.40
  231.5 23.5 %all-to-all-done = bf16[32,16,2048]{2,1,0:T(8,128)(2,1)} async-done(((bf16[32,16,2048]{2,1,0:T(8,128)(2,1)}), bf16[32,16,2048]{2,1,0:T(8,128)(2,1)}, u32[]{:S(2)}, u32[]{:S(2)}) %all-to-all-start) | async-done | bytes 2097184 | tf_op jit(solution)/shard_map/all_to_all | solution.py:122
  255.0 2.4 fusion.80
  257.5 5.1 %fusion.43 = f32[512,2048]{1,0:T(8,128)} fusion(bf16[192,2048]{1,0:T(8,128)(2,1)S(1)} %squeeze.40, bf16[512,2048]{1,0:T(8,128)(2,1)} %bitcast.4, bf16[192,2048]{1,0:T(8,128)(2,1)S(1)} %squeeze.39, f32[512,192]{0,1:T(8,128)S(1)} %fusion.80), kind=kOutput, calls=%fused_computation.42 | convolution fusion | flops 805896192 | bytes 8257536 | tf_op jit(solution)/shard_map/dot_general | solution.py:23
  262.6 0.0 all-gather.6.cloned.1.call-update
  262.6 149.2 %all-gather.6.cloned.1.call-done = f32[2048,2048]{1,0:T(8,128)} async-done(((f32[512,2048]{1,0:T(8,128)}), f32[2048,2048]{1,0:T(8,128)}) %all-gather.6.cloned.1.call-update) | async-done | bytes 16777232 | tf_op jit(solution)/shard_map/all_gather | solution.py:126
  411.8 9.8 %reduce_sum.39 = bf16[512,2048]{1,0:T(8,128)(2,1)} reduce(f32[4,512,2048]{2,1,0:T(8,128)} %bitcast.130, f32[]{:T(128)} %constant.7.clone.1), dimensions={0}, to_apply=%region_7.8 | reduce | flops 3145728 | bytes 18874372 | tf_op jit(solution)/shard_map/reduce_sum | solution.py:126
  421.7 1.9 dynamic-slice_convert_fusion
  423.5 8.2 %all-to-all-start.3 = ((bf16[32,16,512]{2,1,0:T(8,128)(2,1)}), bf16[32,16,512]{2,1,0:T(8,128)(2,1)S(1)}, u32[]{:S(2)}, u32[]{:S(2)}) async-start(bf16[32,16,512]{2,1,0:T(8,128)(2,1)} %bitcast.27), calls=%async_computation.3 | async-start | bytes 1048576 | tf_op jit(solution)/shard_map/all_to_all | solution.py:129
  431.7 0.0 copy-done.1
  431.8 0.0 copy-start.4
  431.8 3.8 copy.39
  435.6 3.8 copy.40
  439.4 3.8 copy.41
  443.3 0.0 all-to-all-done.3
  443.3 1.1 convolution_convert_fusion.2
  (21 shorter events, 0.1 us)
Async XLA Ops:
  7.2 4.1 copy-start.11
  7.2 4.4 copy-start.13
  11.6 2.5 copy-start.9
  14.1 10.7 %copy-start.6 = (f32[1,1024]{1,0:T(1,128)S(1)}, f32[1,1024]{1,0:T(1,128)}, u32[]{:S(2)}) copy-start(f32[1,1024]{1,0:T(1,128)} %param.18) | copy-start | bytes 12292
  14.1 78.2 %copy-start.7 = (s32[1,1024]{1,0:T(1,128)S(1)}, s32[1,1024]{1,0:T(1,128)}, u32[]{:S(2)}) copy-start(s32[1,1024]{1,0:T(1,128)} %param.19) | copy-start | bytes 12292
  93.0 4.0 copy-start.10
  96.9 2.2 copy-start.12
  99.1 1.1 copy-start.15
  151.1 4.5 %copy-start.14 = (s32[32]{0:T(128)S(1)}, s32[32]{0:T(128)}, u32[]{:S(2)}) copy-start(s32[32]{0:T(128)} %param.20) | copy-start | bytes 388
  155.7 12.8 %copy-start.8 = (s32[32]{0:T(128)S(1)}, s32[32]{0:T(128)}, u32[]{:S(2)}) copy-start(s32[32]{0:T(128)} %param.21) | copy-start | bytes 388
  167.0 1.4 copy-start
  177.5 4.8 %copy-start.5 = (s32[256,1]{0,1:T(1,128)S(1)}, s32[256,1]{0,1:T(1,128)}, u32[]{:S(2)}) copy-start(s32[256,1]{0,1:T(1,128)} %param.23) | copy-start | bytes 3076
  177.5 43.8 %all-to-all-start.2 = ((bf16[32,3,6,2048]{3,2,1,0:T(8,128)(2,1)}), bf16[32,3,6,2048]{3,2,1,0:T(8,128)(2,1)S(1)}, u32[]{:S(2)}, u32[]{:S(2)}) async-start(bf16[32,3,6,2048]{3,2,1,0:T(8,128)(2,1)} %copy.38), calls=%async_computation.2 | async-start | bytes 6291456 | tf_op jit(solution)/shard_map/all_to_all | solution.py:104
  181.5 23.6 %all-gather.4.cloned.1.call-start = ((), (), s32[]{:S(2)}) async-start(), calls=%async_computation.4 | async-start | bytes 1310720 | tf_op jit(solution)/shard_map/all_gather | solution.py:117
  221.3 33.7 %all-to-all-start = ((bf16[32,16,2048]{2,1,0:T(8,128)(2,1)}), bf16[32,16,2048]{2,1,0:T(8,128)(2,1)}, u32[]{:S(2)}, u32[]{:S(2)}) async-start(bf16[32,16,2048]{2,1,0:T(8,128)(2,1)} %bitcast.134), calls=%async_computation | async-start | bytes 4194304 | tf_op jit(solution)/shard_map/all_to_all | solution.py:122
  226.6 185.3 %all-gather.6.cloned.1.call-start = ((), (), s32[]{:S(2)}) async-start(), calls=%async_computation.5 | async-start | bytes 20971520 | tf_op jit(solution)/shard_map/all_gather | solution.py:126
  228.3 2.9 copy-start.2
  411.8 19.9 %copy-start.1 = (f32[16,3,1,12288]{3,0,1,2:T(8,128)S(1)}, f32[16,3,1,12288]{3,0,1,2:T(8,128)}, u32[]{:S(2)}) copy-start(f32[16,3,1,12288]{3,0,1,2:T(8,128)} %copy-done) | copy-start | bytes 7077892
  423.5 19.7 %all-to-all-start.3 = ((bf16[32,16,512]{2,1,0:T(8,128)(2,1)}), bf16[32,16,512]{2,1,0:T(8,128)(2,1)S(1)}, u32[]{:S(2)}, u32[]{:S(2)}) async-start(bf16[32,16,512]{2,1,0:T(8,128)(2,1)} %bitcast.27), calls=%async_computation.3 | async-start | bytes 1048576 | tf_op jit(solution)/shard_map/all_to_all | solution.py:129
  431.8 3.8 copy-start.4
  435.6 3.8 copy-start.3
Sparse Core Ops, SparseCore 0:
  184.0 21.0 all-gather.3
  262.7 149.0 all-gather.5
